TPU v7x, 256 devices: a whole 4x4x8 slice. The times are simulated.
256 devices in a mesh: pair: 32 (over z, x), occ: 8 (over y, core).
Axes of the slice: x: 4, y: 4, z: 8, core: 2. Of those that a mesh axis runs over, the one named last changes fastest.
Arguments:
- integrals: bfloat16 [32, 256, 64, 1024], P('pair', None, None, 'occ'), may hold values from -6 to 6
- occ_coeffs: bfloat16 [6144, 128], replicated, may hold values from -0.125 to 0.125
- virt_coeffs: bfloat16 [6144, 5120], P(None, 'pair'), may hold values from -0.078125 to 0.078125
- block_ids: int32 [2, 32, 256], P(None, 'pair'), may hold values from 0 to 95, as said below
- live_mask: int32 [32, 256], P('pair'), may hold values from 0 to 1, as said below
Outputs:
- factors: bfloat16 [128, 16, 5120], P('occ', None, 'pair')
Inputs may be any that keep to these rules, and one draw needn't show every extreme that they name: `block_ids`: slot s of pair index p holds a nu block N with N // 3 == s // 8; each (mu block, nu block) pair is held by at most one slot of all pair indices. `live_mask`: among the 8 slots s with the same s // 8 of one pair index, at most 4 are 1, and exactly 4 for some such group of every pair index.
All inputs are finite; a program needn't handle non-finite values.
Results may differ from a plain program's by a relative error of at most 0.017.
Values may be sent and summed in bfloat16 or wider, within the bound.
A program may use at most 64 MiB of HBM per device.

v0:
```python
import jax
import jax.numpy as jnp
from jax import lax
from jax.sharding import PartitionSpec as P

LIVE = 4


def in_one_piece(arrays, axis, split_dim, concat_dim, along):
    both = jnp.concatenate(arrays, axis=along)
    filled, at, done = (
        lax.all_to_all(both, axis, split_axis=split_dim, concat_axis=concat_dim, tiled=True),
        0,
        [],
    )
    for a in arrays:
        done.append(lax.slice_in_dim(filled, at, at + a.shape[along], axis=along))
        at += a.shape[along]
    return tuple(done)


def half_transform(block_data, mu_index, coeff_blocks):
    slot_count, block_width = (block_data.shape[0], block_data.shape[1])
    aux_local = block_data.shape[2] // block_width
    coeff_rows = jnp.take(coeff_blocks, mu_index, axis=0)
    shaped = block_data.reshape(slot_count, block_width, aux_local, block_width)
    return jnp.einsum("snqm,smi->snqi", shaped, coeff_rows, preferred_element_type=jnp.float32)


def on_device(integrals, occ_coeffs, virt_coeffs, block_ids, live_mask):
    blocks = integrals[0]
    slot_count, block_width = (blocks.shape[0], blocks.shape[1])
    aux_local = blocks.shape[2] // block_width
    occ_count = occ_coeffs.shape[1]
    block_count = occ_coeffs.shape[0] // block_width
    owners = lax.axis_size("pair")
    owned_count = block_count // owners
    group_size = slot_count // owners
    coeff_blocks = occ_coeffs.reshape(block_count, block_width, occ_count)
    mu_index = block_ids[0, 0]
    nu_index = block_ids[1, 0]
    live_flags = live_mask[0]
    grouped_live = live_flags.reshape(owners, group_size)
    sort_keys = (1 - grouped_live) * group_size + jnp.arange(group_size)[None, :]
    chosen = jnp.argsort(sort_keys, axis=1)[:, :LIVE]
    valid_flags = jnp.take_along_axis(grouped_live, chosen, axis=1).reshape(-1)
    slot_index = (chosen + jnp.arange(owners)[:, None] * group_size).reshape(-1)
    send_blocks = blocks[slot_index] * valid_flags[:, None, None].astype(jnp.bfloat16)
    send_blocks = send_blocks.reshape(owners, LIVE, block_width, aux_local * block_width)
    send_mu = mu_index[slot_index].reshape(owners, LIVE)
    send_nu = nu_index[slot_index].reshape(owners, LIVE)
    got_blocks, got_mu, got_nu = (
        lax.all_to_all(send_blocks, "pair", split_axis=0, concat_axis=0, tiled=True),
        *in_one_piece((send_mu, send_nu), "pair", 0, 0, 1),
    )
    partial_terms = half_transform(
        got_blocks.reshape(owners * LIVE, block_width, -1), got_mu.reshape(-1), coeff_blocks
    )
    selector = got_nu.reshape(-1)[None, :] % owned_count == jnp.arange(owned_count)[:, None]
    summed = jnp.dot(
        selector.astype(jnp.float32),
        partial_terms.reshape(owners * LIVE, -1),
        precision=lax.Precision.HIGHEST,
    )
    summed = summed.reshape(owned_count, block_width, aux_local, occ_count)
    half_sums = summed.astype(jnp.bfloat16)
    slab_sums = lax.all_to_all(half_sums, "occ", split_axis=3, concat_axis=2, tiled=True)
    aux_count, slab_rows = (slab_sums.shape[2], slab_sums.shape[3])
    shard_piece = lax.all_gather(slab_sums, "pair", axis=0, tiled=True)
    piece_blocks = shard_piece.shape[0]
    flat_piece = shard_piece.reshape(piece_blocks * block_width, aux_count, slab_rows)
    result = jnp.einsum("nqi,na->iqa", flat_piece, virt_coeffs, preferred_element_type=jnp.float32)
    return result.astype(jnp.bfloat16)


def solution(mesh):
    return jax.shard_map(
        on_device,
        mesh=mesh,
        in_specs=(
            P("pair", None, None, "occ"),
            P(),
            P(None, "pair"),
            P(None, "pair", None),
            P("pair", None),
        ),
        out_specs=P("occ", None, "pair"),
        check_vma=False,
    )
```

profile of v0, /device:TPU:1, one launch (start us, length us, event | category | flops | bytes accessed | tf_op | source)
XLA Modules:
  0.0 251.1 jit_solution(16702428918213110654)
XLA Ops:
  6.5 0.8 fusion.25
  7.9 1.3 reduce.3
  10.3 1.3 gather_fusion.4
  12.0 1.3 gather_fusion.1
  13.2 1.3 gather_fusion
  15.4 11.9 %all-to-all-start = ((s32[32,1,8]{2,1,0:T(1,128)}), s32[32,1,8]{2,1,0:T(1,128)S(1)}, u32[]{:S(2)}, u32[]{:S(2)}) async-start(s32[32,1,8]{2,1,0:T(1,128)} %bitcast.4), calls=%async_computation | async-start | bytes 32768 | tf_op jit(solution)/shard_map/all_to_all | solution.py:12
  27.4 4.3 %gather_fusion.2 = bf16[128,64,128]{2,1,0:T(8,128)(2,1)} fusion(bf16[256,64,128]{2,1,0:T(8,128)(2,1)} %bitcast.62, s32[1024]{0:T(1024)S(1)} %pad_clamp_fusion.1), kind=kCustom, calls=%fused_computation.2 | custom fusion | bytes 4194816 | tf_op jit(solution)/shard_map/gather | solution.py:48
  31.7 3.1 %broadcast_multiply_fusion = bf16[32,4,64,128]{3,2,1,0:T(8,128)(2,1)} fusion(bf16[32,4,64,128]{3,2,1,0:T(8,128)(2,1)} %bitcast.60, bf16[32,4]{1,0:T(8,128)(2,1)S(1)} %copy.55), kind=kLoop, calls=%fused_computation.18 | loop fusion | flops 1048576 | bytes 4194560 | tf_op jit(solution)/shard_map/mul | solution.py:48
  34.8 1.0 all-to-all-done
  35.8 8.5 %all-to-all-start.1 = ((bf16[32,4,64,128]{3,2,1,0:T(8,128)(2,1)}), bf16[32,4,64,128]{3,2,1,0:T(8,128)(2,1)}, u32[]{:S(2)}, u32[]{:S(2)}) async-start(bf16[32,4,64,128]{3,2,1,0:T(8,128)(2,1)} %broadcast_multiply_fusion), calls=%async_computation.1 | async-start | bytes 4194304 | tf_op jit(solution)/shard_map/all_to_all | solution.py:53
  45.1 0.8 reshape.144
  45.9 0.8 reshape.142
  46.7 0.8 rem.20
  47.6 2.2 gather_fusion.3
  49.7 42.5 %all-to-all-done.1 = bf16[32,4,64,128]{3,2,1,0:T(8,128)(2,1)} async-done(((bf16[32,4,64,128]{3,2,1,0:T(8,128)(2,1)}), bf16[32,4,64,128]{3,2,1,0:T(8,128)(2,1)}, u32[]{:S(2)}, u32[]{:S(2)}) %all-to-all-start.1) | async-done | bytes 2097184 | tf_op jit(solution)/shard_map/all_to_all | solution.py:53
  92.3 8.2 %reshape_reshape.3 = bf16[128,64,2,64]{3,2,1,0:T(2,128)(2,1)} reshape(bf16[32,4,64,128]{3,2,1,0:T(8,128)(2,1)} %all-to-all-done.1) | data formatting | bytes 4194304 | tf_op jit(solution)/shard_map/reshape;reshape | solution.py:26
  100.5 7.4 %fusion.2 = f32[128,64,2,128]{3,1,2,0:T(8,128)} fusion(bf16[128,64,2,64]{3,2,1,0:T(2,128)(2,1)} %reshape_reshape.3, bf16[128,64,128]{2,1,0:T(8,128)(2,1)} %gather_fusion.3, pred[128]{0:T(512)(128)(4,1)S(1)} %compare_and_fusion), kind=kOutput, calls=%fused_computation.7 | convolution fusion | flops 269484032 | bytes 12583040 | tf_op jit(solution)/shard_map/snqm,smi->snqi/dot_general | solution.py:27
  107.9 9.2 %copy.57 = f32[128,64,2,128]{0,3,2,1:T(8,128)} copy(f32[128,64,2,128]{3,1,2,0:T(8,128)} %fusion.2) | data formatting | bytes 16777216 | tf_op jit(solution)/shard_map/snqm,smi->snqi/dot_general | solution.py:27
  117.1 7.1 %fusion.12 = bf16[3,64,2,128]{3,0,2,1:T(4,128)(2,1)S(1)} fusion(f32[128,64,2,128]{0,3,2,1:T(8,128)} %copy.57, s32[128]{0:T(128)S(1)} %and_select_fusion), kind=kOutput, calls=%fused_computation.15 | convolution fusion | flops 75547008 | bytes 8487424 | tf_op jit(solution)/shard_map/dot_general | solution.py:60
  124.6 12.4 %all_to_all.35 = bf16[8,2,3072]{2,1,0:T(2,128)(2,1)S(1)} all-to-all(bf16[8,2,3072]{2,1,0:T(2,128)(2,1)S(1)} %reshape.202), channel_id=1, replica_groups=mesh['pair'=32,'occ'=8] {'occ'}, dimensions={0} | all-to-all | bytes 196608 | tf_op jit(solution)/shard_map/all_to_all | solution.py:67
  137.9 84.2 %all-gather.2.cloned.1.call-done = bf16[96,64,16,16]{1,3,2,0:T(8,128)(2,1)} async-done(((bf16[3,64,16,16]{1,3,2,0:T(8,128)(2,1)}), bf16[96,64,16,16]{1,3,2,0:T(8,128)(2,1)}) %all-gather.2.cloned.1.call-update) | async-done | bytes 3145744 | tf_op jit(solution)/shard_map/all_gather | solution.py:69
  222.1 9.5 %copy.61 = bf16[96,64,16,16]{1,0,3,2:T(8,128)(2,1)} copy(bf16[96,64,16,16]{1,3,2,0:T(8,128)(2,1)} %all-gather.2.cloned.1.call-done) | data formatting | bytes 6291456 | tf_op jit(solution)/shard_map/all_gather | solution.py:69
  231.6 9.1 %reshape.146 = bf16[6144,16,16]{0,2,1:T(8,128)(2,1)} reshape(bf16[96,64,16,16]{1,0,3,2:T(8,128)(2,1)} %copy.61) | data formatting | bytes 6291456 | tf_op jit(solution)/shard_map/reshape | solution.py:71
  240.7 2.9 %fusion.15 = bf16[16,16,160]{2,0,1:T(8,128)(2,1)S(1)} fusion(bf16[6144,16,16]{0,2,1:T(8,128)(2,1)} %reshape.146, bf16[6144,160]{0,1:T(8,128)(2,1)S(1)} %copy-done), kind=kOutput, calls=%fused_computation.16 | convolution fusion | flops 503357440 | bytes 5193728 | tf_op jit(solution)/shard_map/nqi,na->iqa/dot_general | solution.py:72
  (38 shorter events, 5.6 us)
Async XLA Ops:
  6.5 234.1 %copy-start = (bf16[6144,160]{0,1:T(8,128)(2,1)S(1)}, bf16[6144,160]{0,1:T(8,128)(2,1)}, u32[]{:S(2)}) copy-start(bf16[6144,160]{0,1:T(8,128)(2,1)} %param.7) | copy-start | bytes 5898244
  15.4 20.4 %all-to-all-start = ((s32[32,1,8]{2,1,0:T(1,128)}), s32[32,1,8]{2,1,0:T(1,128)S(1)}, u32[]{:S(2)}, u32[]{:S(2)}) async-start(s32[32,1,8]{2,1,0:T(1,128)} %bitcast.4), calls=%async_computation | async-start | bytes 32768 | tf_op jit(solution)/shard_map/all_to_all | solution.py:12
  34.8 12.7 %copy-start.1 = (bf16[6144,128]{1,0:T(8,128)(2,1)S(1)}, bf16[6144,128]{1,0:T(8,128)(2,1)}, u32[]{:S(2)}) copy-start(bf16[6144,128]{1,0:T(8,128)(2,1)} %param.6) | copy-start | bytes 4718596
  35.8 56.5 %all-to-all-start.1 = ((bf16[32,4,64,128]{3,2,1,0:T(8,128)(2,1)}), bf16[32,4,64,128]{3,2,1,0:T(8,128)(2,1)}, u32[]{:S(2)}, u32[]{:S(2)}) async-start(bf16[32,4,64,128]{3,2,1,0:T(8,128)(2,1)} %broadcast_multiply_fusion), calls=%async_computation.1 | async-start | bytes 4194304 | tf_op jit(solution)/shard_map/all_to_all | solution.py:53
  44.3 177.8 %all-gather.2.cloned.1.call-start = ((), (), s32[]{:S(2)}) async-start(), calls=%async_computation.3 | async-start | bytes 6488064 | tf_op jit(solution)/shard_map/all_gather | solution.py:69
Sparse Core Ops, SparseCore 0:
  138.0 84.0 all-gather.1
where the time goes:
time: 252 us; the launch traced here: 251 us
  waiting for transfers between devices  128 us (51%)
  local copies, waits for them, and re-layouts  53.1 us (21%)
  starting transfers between devices  20.4 us (8%)
  matrix products  17.4 us (7%)
  between operations  13.6 us (5%)
  blocking collectives  12.4 us (5%)
  other arithmetic  6.55 us (3%)
    all_gather x1, waiting for transfers between devices, on_device(): shard_piece = lax.all_gather(slab_sums, 'pair', axis=0, tiled=True)  84.2 us
    all_to_all x1, waiting for transfers between devices, on_device(): lax.all_to_all(send_blocks, 'pair', split_axis=0, concat_axis=0, tiled=True)  42.5 us
    all_to_all x1, blocking collectives, on_device(): lax.all_to_all(half_sums, 'occ', split_axis=3, concat_axis=2, tiled=True)  12.4 us
    all_to_all x1, starting transfers between devices, in_one_piece(): lax.all_to_all(both, axis, split_axis=split_dim, concat_axis=concat_dim,...  11.9 us
    all_gather x1, local copies, waits for them, and re-layouts, on_device(): shard_piece = lax.all_gather(slab_sums, 'pair', axis=0, tiled=True)  9.49 us
    dot_general x1, local copies, waits for them, and re-layouts, half_transform(): jnp.einsum('snqm,smi->snqi', shaped, coeff_rows, preferred_element_type=j...  9.2 us
    reshape x1, local copies, waits for them, and re-layouts, on_device(): shard_piece.reshape(piece_blocks * block_width, aux_count, slab_rows)  9.09 us
    all_to_all x1, starting transfers between devices, on_device(): lax.all_to_all(send_blocks, 'pair', split_axis=0, concat_axis=0, tiled=True)  8.52 us
  transfers between devices with their start and end apart: 3, of which 3 were waited for; matrix products, arithmetic and copies ran while one was open for 5% of the time, Pallas kernels for 0%

commit v1 on v0

v1 whole, which is shorter than its diff:
```python
import jax
import jax.numpy as jnp
from jax import lax
from jax.experimental import pallas as pl
from jax.experimental.pallas import tpu as pltpu
from jax.sharding import PartitionSpec as P

NZ, NX = 8, 4
OWNERS = NZ * NX
GROUP = 8
OWNED = 3
BS = 64
ROWS = OWNED * BS
CUT = 112
MESH = pl.DeviceIdType.MESH
UP, DOWN = NZ // 2, NZ // 2 - 1


def far_first(k):
    return (NZ // 2 - (k + 1) // 2) * (1 - 2 * (k % 2))


def kernel(
    ids, live, a_hbm, c_hbm, vt_hbm, out,
    a, c, vt, s, h, acc, stage,
    ax2, ax1, axm, bz, bzm, az, azm, bx, bxm,
    ax2_s, ax1_s, axm_s, bz_s, bzm_s, az_s, azm_s, bx_s, bxm_s,
    gaz_s, gazm_s, gax0_s, gax1_s, gaxm_s, gbx_s, gbxm_s, gbz_s, gbzm_s,
    occ_s, in_s,
):
    me, o = lax.axis_index("pair"), lax.axis_index("occ")
    n_occ = lax.axis_size("occ")
    z, x = me // NX, me % NX
    m = 1 - 2 * (o % 2)
    rows_a, rows_b = pl.ds(0, CUT), pl.ds(CUT, ROWS - CUT)

    def zat(d):
        return (z + d * m + NZ) % NZ

    def xat(d):
        return (x + d * m + NX) % NX

    z_up, z_down = zat(1) * NX + x, zat(-1) * NX + x
    x_up, x_down = z * NX + xat(1), z * NX + xat(-1)

    def copy(src, dst, sems, k, to):
        return pltpu.make_async_remote_copy(
            src_ref=src, dst_ref=dst, send_sem=sems.at[0, k], recv_sem=sems.at[1, k],
            device_id={"pair": to}, device_id_type=MESH,
        )

    def load_a(k):
        at = pl.ds(zat(far_first(k)) * NX * GROUP, NX * GROUP)
        return pltpu.make_async_copy(a_hbm.at[at], a.at[at], in_s.at[k])

    load_c = pltpu.make_async_copy(c_hbm, c.at[pl.ds(0, NZ * NX * OWNED)], in_s.at[NZ])
    load_v = pltpu.make_async_copy(vt_hbm, vt, in_s.at[NZ + 1])
    load_c.start()

    @pl.loop(0, NZ)
    def _(k):
        load_a(k).start()

    load_v.start()

    barrier = pltpu.get_barrier_semaphore()
    for to in (z_up, z_down, x_up, x_down):
        pl.semaphore_signal(barrier, inc=1, device_id={"pair": to}, device_id_type=MESH)
    for d in range(1, n_occ):
        pl.semaphore_signal(
            barrier, inc=1, device_id={"occ": (o + d) % n_occ}, device_id_type=MESH
        )
    c[NZ * NX * OWNED] = jnp.zeros((BS, c.shape[2]), c.dtype)
    load_c.wait()

    def ax2_copy(k):
        zz = zat(far_first(k))
        return copy(s.at[zz, xat(2), rows_a], ax2.at[k], ax2_s, k, x_up)

    def ax1_copy(k):
        zz = zat(far_first(k))
        return copy(s.at[zz, xat(1), rows_a], ax1.at[k], ax1_s, k, x_up)

    def axm_copy(k):
        zz = zat(far_first(k))
        return copy(s.at[zz, xat(-1), rows_a], axm.at[k], axm_s, k, x_down)

    def bz_copy(t):
        return copy(s.at[zat(UP - t), :, rows_b], bz.at[t], bz_s, t, z_up)

    def bzm_copy(t):
        return copy(s.at[zat(t - DOWN), :, rows_b], bzm.at[t], bzm_s, t, z_down)

    def az_copy(t):
        return copy(s.at[zat(UP - t), x, rows_a], az.at[t], az_s, t, z_up)

    def azm_copy(t):
        return copy(s.at[zat(t - DOWN), x, rows_a], azm.at[t], azm_s, t, z_down)

    def bx_copy(t):
        return copy(s.at[z, xat(2 - t), rows_b], bx.at[t], bx_s, t, x_up)

    bxm_copy = copy(s.at[z, xat(-1), rows_b], bxm, bxm_s, 0, x_down)

    def add(at, *terms):
        total = s[at].astype(jnp.float32)
        for t in terms:
            total += t.astype(jnp.float32)
        s[at] = total.astype(s.dtype)

    def transform(zz, xx):
        q = zz * NX + xx
        left, right, picks = [], [], [[] for _ in range(OWNED)]
        for j in range(GROUP // 2):
            even, odd = a[q * GROUP + 2 * j], a[q * GROUP + 2 * j + 1]
            left.append(jnp.concatenate([even[:, :BS], odd[:, :BS]], axis=1))
            right.append(jnp.concatenate([even[:, BS:], odd[:, BS:]], axis=1))
        for j in range(GROUP):
            slot = q * GROUP + j
            mu, nu, on = ids[0, 0, slot], ids[1, 0, slot], live[0, slot]
            for b in range(OWNED):
                hit = jnp.logical_and(on != 0, nu == q * OWNED + b)
                picks[b].append(c[jnp.where(hit, mu, NZ * NX * OWNED)])
        lhs = jnp.concatenate(
            [jnp.concatenate(left, axis=1), jnp.concatenate(right, axis=1)], axis=0
        )
        rhs = jnp.concatenate([jnp.concatenate(p, axis=0) for p in picks], axis=1)
        got = jnp.dot(lhs, rhs, preferred_element_type=jnp.float32).astype(s.dtype)
        n_i = c.shape[2]
        for b in range(OWNED):
            for side in range(2):
                s[zz, xx, pl.ds(b * BS, BS), pl.ds(side * n_i, n_i)] = got[
                    side * BS : (side + 1) * BS, b * n_i : (b + 1) * n_i
                ]

    @pl.loop(0, NZ)
    def _(k):
        zz = zat(far_first(k))
        load_a(k).wait()

        @pl.loop(0, NX)
        def _(xx):
            transform(zz, xx)

        @pl.when(k == 0)
        def _():
            pl.semaphore_wait(barrier, 4 + n_occ - 1)

        ax2_copy(k).start()
        axm_copy(k).start()

        @pl.when(k == 0)
        def _():
            bz_copy(0).start()

        @pl.when(k == 1)
        def _():
            bzm_copy(0).start()

    def bz_step(t):
        bz_copy(t).wait_recv()
        add((zat(UP - 1 - t), slice(None), rows_b), bz[t])
        bz_copy(t + 1).start()

    def bzm_step(t):
        bzm_copy(t).wait_recv()
        add((zat(t + 1 - DOWN), slice(None), rows_b), bzm[t])
        bzm_copy(t + 1).start()

    def az_step(t):
        az_copy(t).wait_recv()
        add((zat(UP - 1 - t), x, rows_a), az[t])
        az_copy(t + 1).start()

    def azm_step(t):
        azm_copy(t).wait_recv()
        add((zat(t + 1 - DOWN), x, rows_a), azm[t])
        azm_copy(t + 1).start()

    def ax_steps(lo, hi):
        @pl.loop(lo, hi)
        def _(k):
            ax2_copy(k).wait_recv()
            add((zat(far_first(k)), xat(1), rows_a), ax2[k])
            ax1_copy(k).start()

    bz_step(0)
    bzm_step(0)
    ax_steps(0, 3)
    bz_step(1)
    bzm_step(1)
    ax_steps(3, 6)
    bz_step(2)
    ax_steps(6, 8)
    bzm_copy(2).wait_recv()
    bz_copy(3).wait_recv()
    add((z, slice(None), rows_b), bz[3], bzm[2])
    bx_copy(0).start()
    bxm_copy.start()

    @pl.loop(0, NZ)
    def _(k):
        ax1_copy(k).wait_recv()
        axm_copy(k).wait_recv()
        add((zat(far_first(k)), x, rows_a), ax1[k], axm[k])

        @pl.when(k == 0)
        def _():
            az_copy(0).start()

        @pl.when(k == 1)
        def _():
            azm_copy(0).start()

    bx_copy(0).wait_recv()
    add((z, xat(1), rows_b), bx[0])
    bx_copy(1).start()
    az_step(0)
    azm_step(0)
    bxm_copy.wait_recv()
    bx_copy(1).wait_recv()

    def gaz_copy(t):
        part = h.at[zat(-t), x, rows_a]
        return copy(part, part, gaz_s, t, z_up)

    def gazm_copy(t):
        part = h.at[zat(t), x, rows_a]
        return copy(part, part, gazm_s, t, z_down)

    def gax0_copy(k):
        part = h.at[zat(far_first(NZ - 1 - k)), x, rows_a]
        return copy(part, part, gax0_s, k, x_up)

    def gax1_copy(k):
        part = h.at[zat(far_first(NZ - 1 - k)), xat(-1), rows_a]
        return copy(part, part, gax1_s, k, x_up)

    def gaxm_copy(k):
        part = h.at[zat(far_first(NZ - 1 - k)), x, rows_a]
        return copy(part, part, gaxm_s, k, x_down)

    def gbx_copy(t):
        part = h.at[z, xat(-t), rows_b]
        return copy(part, part, gbx_s, t, x_up)

    own_b = h.at[z, x, rows_b]
    gbxm_copy = copy(own_b, own_b, gbxm_s, 0, x_down)

    def gbz_copy(t):
        part = h.at[zat(-t), :, rows_b]
        return copy(part, part, gbz_s, t, z_up)

    def gbzm_copy(t):
        part = h.at[zat(t), :, rows_b]
        return copy(part, part, gbzm_s, t, z_down)

    def own(rows, *terms):
        total = s[z, x, rows].astype(jnp.float32)
        for t in terms:
            total += t.astype(jnp.float32)
        h[z, x, rows] = total.astype(h.dtype)

    own(rows_b, bx[1], bxm[...])
    gbx_copy(0).start()
    gbxm_copy.start()
    az_step(1)
    azm_step(1)
    az_step(2)
    gbx_copy(0).wait_recv()
    gbx_copy(1).start()
    gbxm_copy.wait_recv()
    azm_copy(2).wait_recv()
    az_copy(3).wait_recv()
    own(rows_a, az[3], azm[2])
    gaz_copy(0).start()
    gazm_copy(0).start()
    gax0_copy(0).start()
    gaxm_copy(0).start()
    gbx_copy(1).wait_recv()
    gbz_copy(0).start()
    gbzm_copy(0).start()

    @pl.loop(0, NZ)
    def _(k):
        ax2_copy(k).wait_send()
        ax1_copy(k).wait_send()
        axm_copy(k).wait_send()

    for t in range(UP):
        bz_copy(t).wait_send()
        az_copy(t).wait_send()
    for t in range(DOWN):
        bzm_copy(t).wait_send()
        azm_copy(t).wait_send()
    bx_copy(0).wait_send()
    bx_copy(1).wait_send()
    bxm_copy.wait_send()
    load_v.wait()

    def gaz_step(t):
        gaz_copy(t).wait_recv()
        if t + 1 < UP:
            gaz_copy(t + 1).start()
        k = 2 * t + 2 if t + 1 < UP else NZ - 1
        gax0_copy(gather_at(-(t + 1))).start()
        gaxm_copy(gather_at(-(t + 1))).start()
        del k

    def gazm_step(t):
        gazm_copy(t).wait_recv()
        if t + 1 < DOWN:
            gazm_copy(t + 1).start()
        gax0_copy(gather_at(t + 1)).start()
        gaxm_copy(gather_at(t + 1)).start()

    def gather_at(d):
        return [far_first(NZ - 1 - k) % NZ for k in range(NZ)].index(d % NZ)

    def gbz_step(t):
        gbz_copy(t).wait_recv()
        if t + 1 < UP:
            gbz_copy(t + 1).start()

    def gbzm_step(t):
        gbzm_copy(t).wait_recv()
        if t + 1 < DOWN:
            gbzm_copy(t + 1).start()

    def gax_steps(lo, hi):
        @pl.loop(lo, hi)
        def _(k):
            gax0_copy(k).wait_recv()
            gax1_copy(k).start()

    def multiply(k):
        gax1_copy(k).wait_recv()
        gaxm_copy(k).wait_recv()
        zz = zat(far_first(NZ - 1 - k))
        depth = NX * ROWS
        at = pl.ds(pl.multiple_of(zz * depth, 128), depth)
        acc[...] += jnp.dot(
            vt[:, at], h[zz].reshape(depth, h.shape[3]), preferred_element_type=jnp.float32
        )

    acc[...] = jnp.zeros_like(acc)
    gaz_step(0)
    gazm_step(0)
    gax_steps(0, 1)
    gaz_step(1)
    gazm_step(1)
    gbz_step(0)
    gbzm_step(0)
    gaz_step(2)
    gazm_step(2)
    gaz_step(3)
    gax_steps(1, 3)
    gbz_step(1)
    gbzm_step(1)
    gax_steps(3, 5)
    gbz_step(2)
    gbzm_step(2)
    gax_steps(5, 8)

    @pl.loop(0, NZ - 1)
    def _(k):
        multiply(k)

    gbz_step(3)
    multiply(NZ - 1)

    turned = acc[...].T.astype(stage.dtype)
    part = stage.shape[2]
    for side in range(2):
        for d in range(n_occ):
            at = (side * n_occ + d) * part
            stage[d, side] = turned[at : at + part]

    def occ_copy(d):
        return pltpu.make_async_remote_copy(
            src_ref=stage.at[(o + d) % n_occ], dst_ref=out.at[pl.ds(2 * o, 2)],
            send_sem=occ_s.at[0, d], recv_sem=occ_s.at[1, d],
            device_id={"occ": (o + d) % n_occ}, device_id_type=MESH,
        )

    for d in range(1, n_occ):
        occ_copy(d).start()
    mine = pltpu.make_async_copy(stage.at[o], out.at[pl.ds(2 * o, 2)], occ_s.at[0, 0])
    mine.start()

    @pl.loop(0, NZ)
    def _(k):
        gax0_copy(k).wait_send()
        gax1_copy(k).wait_send()
        gaxm_copy(k).wait_send()

    for t in range(UP):
        gaz_copy(t).wait_send()
        gbz_copy(t).wait_send()
    for t in range(DOWN):
        gazm_copy(t).wait_send()
        gbzm_copy(t).wait_send()
    gbx_copy(0).wait_send()
    gbx_copy(1).wait_send()
    gbxm_copy.wait_send()
    mine.wait()
    for d in range(1, n_occ):
        occ_copy(d).wait_send()
        src = (o + n_occ - d) % n_occ
        pltpu.make_async_remote_copy(
            src_ref=stage.at[src], dst_ref=out.at[pl.ds(2 * src, 2)],
            send_sem=occ_s.at[0, d], recv_sem=occ_s.at[1, d],
            device_id={"occ": src}, device_id_type=MESH,
        ).wait_recv()


def on_device(integrals, occ_coeffs, virt_coeffs, block_ids, live_mask):
    blocks = integrals[0]
    n_i = occ_coeffs.shape[1]
    n_a = virt_coeffs.shape[1]
    n_occ = lax.axis_size("occ")
    bf16, f32 = jnp.bfloat16, jnp.float32
    wide = 2 * n_i
    ra, rb = CUT, ROWS - CUT
    any_space, smem = pl.BlockSpec(memory_space=pl.ANY), pl.BlockSpec(memory_space=pltpu.SMEM)

    def sems(k):
        return pltpu.SemaphoreType.DMA((2, k))

    got = pl.pallas_call(
        kernel,
        out_shape=jax.ShapeDtypeStruct((2 * n_occ, n_i // n_occ, n_a), bf16),
        in_specs=[smem, smem, any_space, any_space, any_space],
        out_specs=pl.BlockSpec(memory_space=pltpu.VMEM),
        scratch_shapes=[
            pltpu.VMEM(blocks.shape, bf16),
            pltpu.VMEM((OWNERS * OWNED + 1, BS, n_i), bf16),
            pltpu.VMEM((n_a, OWNERS * ROWS), bf16),
            pltpu.VMEM((NZ, NX, ROWS, wide), bf16),
            pltpu.VMEM((NZ, NX, ROWS, wide), bf16),
            pltpu.VMEM((n_a, wide), f32),
            pltpu.VMEM((n_occ, 2, n_i // n_occ, n_a), bf16),
            pltpu.VMEM((NZ, ra, wide), bf16),
            pltpu.VMEM((NZ, ra, wide), bf16),
            pltpu.VMEM((NZ, ra, wide), bf16),
            pltpu.VMEM((UP, NX, rb, wide), bf16),
            pltpu.VMEM((DOWN, NX, rb, wide), bf16),
            pltpu.VMEM((UP, ra, wide), bf16),
            pltpu.VMEM((DOWN, ra, wide), bf16),
            pltpu.VMEM((2, rb, wide), bf16),
            pltpu.VMEM((rb, wide), bf16),
            sems(NZ), sems(NZ), sems(NZ), sems(UP), sems(DOWN), sems(UP), sems(DOWN), sems(2), sems(1),
            sems(UP), sems(DOWN), sems(NZ), sems(NZ), sems(NZ), sems(2), sems(1), sems(UP), sems(DOWN),
            sems(n_occ),
            pltpu.SemaphoreType.DMA((NZ + 2,)),
        ],
        compiler_params=pltpu.CompilerParams(
            collective_id=0, has_side_effects=True, vmem_limit_bytes=48 << 20
        ),
    )(
        block_ids,
        live_mask,
        blocks,
        occ_coeffs.reshape(OWNERS * OWNED, BS, n_i),
        virt_coeffs.T,
    )
    return jnp.transpose(got, (1, 0, 2))


def solution(mesh):
    return jax.shard_map(
        on_device,
        mesh=mesh,
        in_specs=(
            P("pair", None, None, "occ"),
            P(),
            P(None, "pair"),
            P(None, "pair", None),
            P("pair", None),
        ),
        out_specs=P("occ", None, "pair"),
        check_vma=False,
    )
```

time: 252 us -> 83.6 us (0.33)
  waiting for transfers between devices: 128 us -> 0 us
  Pallas kernels: 0 us -> 78.4 us
  local copies, waits for them, and re-layouts: 53.1 us -> 5.01 us
  starting transfers between devices: 20.4 us -> 0 us
  matrix products: 17.4 us -> 0 us
  between operations: 13.6 us -> 0.01 us
  blocking collectives: 12.4 us -> 0 us
  other arithmetic: 6.55 us -> 0 us
    all_gather x1 -> x0, waiting for transfers between devices: 84.2 us -> none  [on_device(): shard_piece = lax.all_gather(slab_sums, 'pair', axis=0, tiled=True)]
    pallas_call x0 -> x1, Pallas kernels: none -> 78.4 us  [on_device(): pl.pallas_call(kernel, out_shape=jax.ShapeDtypeStruct((2 * n_occ, n_i //...]
    all_to_all x2 -> x0, waiting for transfers between devices: 43.5 us -> none  [the longest x1 42.5 us: on_device(): lax.all_to_all(send_blocks, 'pair', split_axis=0, concat_axis=0, tiled=True)]
    all_to_all x2 -> x0, starting transfers between devices: 20.4 us -> none  [the longest x1 11.9 us: in_one_piece(): lax.all_to_all(both, axis, split_axis=split_dim, concat_axis=concat_dim,...]
    dot_general x3 -> x0, matrix products: 17.4 us -> none  [the longest x1 7.39 us: half_transform(): jnp.einsum('snqm,smi->snqi', shaped, coeff_rows, preferred_element_type=j...]
    all_to_all x1 -> x0, blocking collectives: 12.4 us -> none  [on_device(): lax.all_to_all(half_sums, 'occ', split_axis=3, concat_axis=2, tiled=True)]
    reshape x6 -> x0, local copies, waits for them, and re-layouts: 11 us -> none  [the longest x1 9.09 us: on_device(): shard_piece.reshape(piece_blocks * block_width, aux_count, slab_rows)]
    gather x9 -> x0, local copies, waits for them, and re-layouts: 10.7 us -> none  [the longest x1 4.35 us: on_device(): blocks[slot_index] * valid_flags[:, None, None].astype(jnp.bfloat16)]
  transfers between devices with their start and end apart: 3 -> 0, of which waited for: 3 -> 0; matrix products, arithmetic and copies ran while one was open for 5% -> 0% of each run, Pallas kernels for 0% -> 0%
where the time goes in v1:
time: 83.6 us; the launch traced here: 83.5 us
  Pallas kernels  78.4 us (94%)
  local copies, waits for them, and re-layouts  5.01 us (6%)
    pallas_call x1, Pallas kernels, on_device(): pl.pallas_call(kernel, out_shape=jax.ShapeDtypeStruct((2 * n_occ, n_i //...  78.4 us
    unnamed x8, local copies, waits for them, and re-layouts  4.31 us

profile of v1, /device:TPU:1, one launch (start us, length us, event | category | flops | bytes accessed | tf_op | source)
XLA Modules:
  0.0 83.5 jit_solution(5262086715754334452)
XLA Ops:
  0.0 0.0 copy-start
  0.0 1.5 %copy-done = bf16[6144,160]{0,1:T(8,128)(2,1)S(1)} copy-done((bf16[6144,160]{0,1:T(8,128)(2,1)S(1)}, bf16[6144,160]{0,1:T(8,128)(2,1)}, u32[]{:S(2)}) %copy-start) | copy-done | bytes 1966104
  1.5 0.0 copy-start.1
  1.5 1.4 %copy-done.1 = bf16[6144,128]{1,0:T(8,128)(2,1)S(1)} copy-done((bf16[6144,128]{1,0:T(8,128)(2,1)S(1)}, bf16[6144,128]{1,0:T(8,128)(2,1)}, u32[]{:S(2)}) %copy-start.1) | copy-done | bytes 1572888
  3.0 0.0 copy-start.2
  3.0 0.7 copy-done.2
  3.6 0.0 copy-start.3
  3.6 0.7 copy-done.3
  4.3 78.4 %shard_map.55 = bf16[16,16,160]{2,1,0:T(8,128)(2,1)S(1)} custom-call(s32[2,1,256]{2,1,0:T(1,128)S(1)} %copy-done.2, s32[1,256]{1,0:T(1,128)S(1)} %copy-done.3, bf16[256,64,128]{2,1,0:T(8,128)(2,1)} %bitcast.7, bf16[96,64,128]{2,1,0:T(8,128)(2,1)S(1)} %bitcast.5, bf16[160,6144]{1,0:T(8,128)(2,1)S(1)} %bitcast.4), custom_call_target="tpu_custom_call" | custom-call | tf_op jit(solution)/shard_map/pallas_call | solution.py:430
  82.8 0.7 copy.6
Async XLA Ops:
  0.0 1.5 %copy-start = (bf16[6144,160]{0,1:T(8,128)(2,1)S(1)}, bf16[6144,160]{0,1:T(8,128)(2,1)}, u32[]{:S(2)}) copy-start(bf16[6144,160]{0,1:T(8,128)(2,1)} %param.7) | copy-start | bytes 5898244
  1.5 1.4 %copy-start.1 = (bf16[6144,128]{1,0:T(8,128)(2,1)S(1)}, bf16[6144,128]{1,0:T(8,128)(2,1)}, u32[]{:S(2)}) copy-start(bf16[6144,128]{1,0:T(8,128)(2,1)} %param.6) | copy-start | bytes 4718596
  3.0 0.7 copy-start.2
  3.6 0.7 copy-start.3

commit v2 on v0

v2 whole, which is shorter than its diff:
```python
import jax
import jax.numpy as jnp
from jax import lax
from jax.experimental import pallas as pl
from jax.experimental.pallas import tpu as pltpu
from jax.sharding import PartitionSpec as P

NZ, NX = 8, 4
OWNERS = NZ * NX
GROUP = 8
LIVE = 4
OWNED = 3
BS = 64
ROWS = OWNED * BS
CUT = 112
UP, DOWN = NZ // 2, NZ // 2 - 1
MESH = pl.DeviceIdType.MESH
FIRST = ((0, 2), (2, 5), (5, 8))
HALVES = 2

RATE, LATENCY, HOP, WINDOW = 88e3, 1.25, 0.65, 1.5


def far_first(k):
    return (NZ // 2 - (k + 1) // 2) * (1 - 2 * (k % 2))


class Step:
    def __init__(self, name, cost, after, needs, sends, run):
        self.name, self.cost, self.after, self.needs, self.sends, self.run = name, cost, after, needs, sends, run


def in_order(steps):
    by_name = {s.name: s for s in steps}
    maker = {m[0]: (s, m) for s in steps for m in s.sends}
    follow = {s.name: [] for s in steps}
    for s in steps:
        for p in s.after:
            follow[p].append((s.name, 0.0))
        for n in s.needs:
            p, (_, _, size, hops) = maker[n]
            follow[p.name].append((s.name, LATENCY + HOP * hops + size * hops / RATE))
    ranks = {}

    def rank(n):
        if n not in ranks:
            ranks[n] = by_name[n].cost + max([c + rank(f) for f, c in follow[n]], default=0.0)
        return ranks[n]

    done, there, free, gone = {}, {}, {"x": 0.0, "z": 0.0}, {}
    now, left, out = 0.0, list(steps), []
    while left:
        best, later = None, []
        for s in left:
            if any(p not in done for p in s.after) or any(n not in there for n in s.needs):
                continue
            at = max([done[p] for p in s.after] + [there[n] for n in s.needs] + [0.0])
            at = max([at] + [free[link] - WINDOW for _, link, _, _ in s.sends])
            if at > now + 1e-9:
                later.append(at)
            elif best is None or rank(s.name) > rank(best.name):
                best = s
        if best is None:
            now = min(later)
            continue
        left.remove(best)
        now += best.cost
        done[best.name] = now
        for n, link, size, hops in best.sends:
            free[link] = max(now, free[link]) + size * hops / RATE
            there[n] = free[link] + LATENCY + HOP * hops
            gone[n] = there[n] + 4.0
        past = [n for n in gone if gone[n] < now]
        for n in past:
            del gone[n]
        out.append((best, past))
    out.append((None, list(gone)))
    return out


def kernel(
    ids, live, a_hbm, c_hbm, vt_hbm, out,
    a0, a1, a2, c, vt, s, h, acc, stage,
    ax2, ax1, axm, az, azm, bz, bzm, bx,
    sems, occ_s, in_s,
):
    me, o = lax.axis_index("pair"), lax.axis_index("occ")
    n_occ = lax.axis_size("occ")
    z, x = me // NX, me % NX
    m = 1 - 2 * (o % 2)
    n_i = c.shape[2]
    rows_a, rows_b = pl.ds(0, CUT), pl.ds(CUT, ROWS - CUT)

    def zat(d):
        return (z + d * m + NZ) % NZ

    def xat(d):
        return (x + d * m + NX) % NX

    z_up, z_down = zat(1) * NX + x, zat(-1) * NX + x
    x_up, x_down, x_far = z * NX + xat(1), z * NX + xat(-1), z * NX + xat(2)

    parts = (a0, a1, a2)
    slots = NX * GROUP

    def load_a(g, k):
        return pltpu.make_async_copy(
            a_hbm.at[pl.ds(zat(far_first(k)) * slots, slots)],
            parts[g].at[pl.ds((k - FIRST[g][0]) * slots, slots)],
            in_s.at[k],
        )

    load_c = pltpu.make_async_copy(c_hbm, c.at[pl.ds(0, OWNERS * OWNED)], in_s.at[NZ])
    load_v = pltpu.make_async_copy(vt_hbm, vt, in_s.at[NZ + 1])
    load_c.start()
    for g, (lo, hi) in enumerate(FIRST):
        for k in range(lo, hi):
            load_a(g, k).start()
    load_v.start()

    barrier = pltpu.get_barrier_semaphore()
    for to in (z_up, z_down, x_up, x_down, x_far):
        pl.semaphore_signal(barrier, inc=1, device_id={"pair": to}, device_id_type=MESH)
    for d in range(1, n_occ):
        pl.semaphore_signal(
            barrier, inc=1, device_id={"occ": (o + d) % n_occ}, device_id_type=MESH
        )
    c[OWNERS * OWNED] = jnp.zeros((BS, n_i), c.dtype)
    load_c.wait()

    def transform(part, at, q):
        on = [live[0, q * GROUP + j] for j in range(GROUP)]
        seen, before = 0, []
        for j in range(GROUP):
            before.append(seen)
            seen = seen + on[j]
        blocks, picks = [], [[] for _ in range(OWNED)]
        for n in range(LIVE):
            slot = 0
            for j in range(1, GROUP):
                slot = slot + jnp.where(jnp.logical_and(on[j] != 0, before[j] == n), j, 0)
            mu, nu = ids[0, 0, q * GROUP + slot], ids[1, 0, q * GROUP + slot]
            blocks.append(part[at + slot])
            for b in range(OWNED):
                hit = jnp.logical_and(seen > n, nu == q * OWNED + b)
                picks[b].append(c[jnp.where(hit, mu, OWNERS * OWNED)])
        left = [t[:, :BS] for t in blocks]
        right = [t[:, BS:] for t in blocks]
        lhs = jnp.concatenate(
            [jnp.concatenate(left, axis=1), jnp.concatenate(right, axis=1)], axis=0
        )
        rhs = jnp.concatenate([jnp.concatenate(p, axis=0) for p in picks], axis=1)
        got = jnp.dot(lhs, rhs, preferred_element_type=jnp.float32).astype(s.dtype)
        for b in range(OWNED):
            for side in range(2):
                s[q // NX, q % NX, pl.ds(b * BS, BS), pl.ds(side * n_i, n_i)] = got[
                    side * BS : (side + 1) * BS, b * n_i : (b + 1) * n_i
                ]

    copies, numbers = {}, {}

    def message(name, to, src, dst):
        numbers[name] = len(numbers)

        def make():
            return pltpu.make_async_remote_copy(
                src_ref=src(), dst_ref=dst(),
                send_sem=sems.at[0, numbers[name]], recv_sem=sems.at[1, numbers[name]],
                device_id={"pair": to}, device_id_type=MESH,
            )

        copies[name] = make

    def stay(name, to, part):
        message(name, to, part, part)

    steps = []
    one_a, one_b = CUT * s.shape[3] * 2, (ROWS - CUT) * s.shape[3] * 2
    start_cost = 0.04

    def add_cost(size):
        return 0.05 + size / 4e5

    def step(name, after=(), needs=(), sends=(), run=lambda: None, cost=start_cost):
        steps.append(Step(name, cost, list(after), list(needs), list(sends), run))

    def add(at, *terms, into=s):
        def run():
            total = s[at].astype(jnp.float32)
            for t in terms:
                total += t().astype(jnp.float32)
            into[at] = total.astype(into.dtype)

        return run

    place = {far_first(k): k for k in range(NZ)}
    ready = {k: ("transform", g) for g, (lo, hi) in enumerate(FIRST) for k in range(lo, hi)}

    def run_transform(g):
        lo, hi = FIRST[g]

        def run():
            for k in range(lo, hi):
                load_a(g, k).wait()

            @pl.loop(0, (hi - lo) * NX)
            def _(n):
                q = zat(far_first(lo + n // NX)) * NX + n % NX
                transform(parts[g], n * GROUP, q)

            if g == 0:
                pl.semaphore_wait(barrier, 5 + n_occ - 1)

        return run

    for g, (lo, hi) in enumerate(FIRST):
        step(
            ready[lo], [("transform", g - 1)] if g else [], run=run_transform(g),
            cost=0.55 * (hi - lo) + (2.0 if g == 0 else 0.0),
        )

    for k in range(NZ):
        d = far_first(k)
        message(("ax2", k), x_up, lambda d=d: s.at[zat(d), xat(2), rows_a], lambda k=k: ax2.at[k])
        message(("ax1", k), x_up, lambda d=d: s.at[zat(d), xat(1), rows_a], lambda k=k: ax1.at[k])
        message(("axm", k), x_down, lambda d=d: s.at[zat(d), xat(-1), rows_a], lambda k=k: axm.at[k])
        step(("ax2", k), [ready[k]], [], [(("ax2", k), "x", one_a, 1)])
        step(("axm", k), [ready[k]], [], [(("axm", k), "x", one_a, 1)])
        step(
            ("ax1", k), [ready[k]], [("ax2", k)], [(("ax1", k), "x", one_a, 1)],
            add((zat(d), xat(1), rows_a), lambda k=k: ax2[k]), add_cost(one_a),
        )
        step(
            ("ax", k), [ready[k]], [("ax1", k), ("axm", k)], [],
            add((zat(d), x, rows_a), lambda k=k: ax1[k], lambda k=k: axm[k]), 1.3 * add_cost(one_a),
        )

    for f in range(HALVES):
        lanes = pl.ds(f * n_i, n_i)
        size = one_a // HALVES
        for kind, hops, to, buf, sign in (("az", UP, z_up, az, 1), ("azm", DOWN, z_down, azm, -1)):
            for t in range(hops):
                d = sign * (hops - t)
                message(
                    (kind, t, f), to,
                    lambda d=d, lanes=lanes: s.at[zat(d), x, rows_a, lanes],
                    lambda t=t, lanes=lanes, buf=buf: buf.at[t, :, lanes],
                )
                if t:
                    run = add((zat(d), x, rows_a, lanes), lambda t=t, lanes=lanes, buf=buf: buf[t - 1, :, lanes])
                else:
                    run = lambda: None
                step(
                    (kind, t, f), [("ax", place[d])], [(kind, t - 1, f)] if t else [],
                    [((kind, t, f), "z", size, 1)], run, add_cost(size) if t else start_cost,
                )
        step(
            ("own a", f), [("ax", place[0])], [("az", UP - 1, f), ("azm", DOWN - 1, f)], [],
            add(
                (z, x, rows_a, lanes),
                lambda lanes=lanes: az[UP - 1, :, lanes], lambda lanes=lanes: azm[DOWN - 1, :, lanes], into=h,
            ), 1.5 * add_cost(size),
        )

    for j, dx in enumerate((2, 1, -1, 0)):
        for kind, hops, to, buf, sign in (("bz", UP, z_up, bz, 1), ("bzm", DOWN, z_down, bzm, -1)):
            for t in range(hops):
                d = sign * (hops - t)
                message(
                    (kind, t, j), to,
                    lambda d=d, dx=dx: s.at[zat(d), xat(dx), rows_b],
                    lambda t=t, j=j, buf=buf: buf.at[t, j],
                )
                if t:
                    run = add((zat(d), xat(dx), rows_b), lambda t=t, j=j, buf=buf: buf[t - 1, j])
                else:
                    run = lambda: None
                step(
                    (kind, t, j), [ready[place[d]]], [(kind, t - 1, j)] if t else [],
                    [((kind, t, j), "z", one_b, 1)], run, add_cost(one_b) if t else start_cost,
                )
        if dx:
            to = {2: x_far, 1: x_up, -1: x_down}[dx]
            message(("bx", j), to, lambda dx=dx: s.at[z, xat(dx), rows_b], lambda j=j: bx.at[j])
        step(
            ("b", j), [ready[place[0]]], [("bz", UP - 1, j), ("bzm", DOWN - 1, j)],
            [(("bx", j), "x", one_b, abs(dx))] if dx else [],
            add((z, xat(dx), rows_b), lambda j=j: bz[UP - 1, j], lambda j=j: bzm[DOWN - 1, j]), 1.3 * add_cost(one_b),
        )

    for j, (to, dx) in enumerate(((x_far, 2), (x_up, 1), (x_down, 1))):
        stay(("gb", j), to, lambda: h.at[z, x, rows_b])
    step(
        ("own b",), [("b", 3)], [("bx", j) for j in range(3)],
        [(("gb", 0), "x", one_b, 2), (("gb", 1), "x", one_b, 1), (("gb", 2), "x", one_b, 1)],
        add((z, x, rows_b), lambda: bx[0], lambda: bx[1], lambda: bx[2], into=h), 2 * add_cost(one_b),
    )
    for j, dx in enumerate((2, -1, 1, 0)):
        for kind, hops, to, sign in (("gbz", UP, z_up, -1), ("gbzm", DOWN, z_down, 1)):
            for t in range(hops):
                stay((kind, t, j), to, lambda t=t, dx=dx, sign=sign: h.at[zat(sign * t), xat(dx), rows_b])
                needs = [(kind, t - 1, j)] if t else ([("gb", j)] if dx else [])
                step((kind, t, j), [] if t or dx else [("own b",)], needs, [((kind, t, j), "z", one_b, 1)])
    for f in range(HALVES):
        lanes = pl.ds(f * n_i, n_i)
        for kind, hops, to, sign in (("gaz", UP, z_up, -1), ("gazm", DOWN, z_down, 1)):
            for t in range(hops):
                stay(
                    (kind, t, f), to,
                    lambda t=t, sign=sign, lanes=lanes: h.at[zat(sign * t), x, rows_a, lanes],
                )
                step(
                    (kind, t, f), [] if t else [("own a", f)], [(kind, t - 1, f)] if t else [],
                    [((kind, t, f), "z", one_a // HALVES, 1)],
                )
    for k in reversed(range(NZ)):
        d = far_first(k) if k else -UP
        after = [("own a", f) for f in range(HALVES)] if d == 0 else []
        halves = range(HALVES) if d else []
        came = [("gaz", -d - 1, f) if d < 0 else ("gazm", d - 1, f) for f in halves]
        stay(("gax0", d), x_up, lambda d=d: h.at[zat(d), x, rows_a])
        stay(("gaxm", d), x_down, lambda d=d: h.at[zat(d), x, rows_a])
        stay(("gax1", d), x_up, lambda d=d: h.at[zat(d), xat(-1), rows_a])
        step(("gax0", d), after, came, [(("gax0", d), "x", one_a, 1)])
        step(("gaxm", d), after, came, [(("gaxm", d), "x", one_a, 1)])
        step(("gax1", d), [], [("gax0", d)], [(("gax1", d), "x", one_a, 1)])

    def multiply(d):
        def run():
            depth = NX * ROWS
            zz = zat(d)
            at = pl.ds(pl.multiple_of(zz * depth, 128), depth)
            acc[...] += jnp.dot(
                vt[:, at], h[zz].reshape(depth, h.shape[3]), preferred_element_type=jnp.float32
            )

        return run

    def clear():
        load_v.wait()
        acc[...] = jnp.zeros_like(acc)

    step(("clear",), [("own b",)], run=clear, cost=0.2)
    for k in reversed(range(NZ)):
        d = far_first(k) if k else -UP
        needs = [("gax0", d), ("gax1", d), ("gaxm", d)]
        if d == 0:
            needs += [("gb", j) for j in range(3)]
        else:
            needs += [("gbz", -d - 1, j) if d < 0 else ("gbzm", d - 1, j) for j in range(NX)]
        step(
            ("multiply", d), [("clear",)] + ([("own a", f) for f in range(HALVES)] if d == 0 else []), needs,
            run=multiply(d), cost=0.3,
        )

    waited, last = set(), []
    for st, past in in_order(steps):
        if st is None:
            last = past
            continue
        for n in st.needs:
            if n not in waited:
                waited.add(n)
                copies[n]().wait_recv()
        st.run()
        for n, _, _, _ in st.sends:
            copies[n]().start()
        for n in past:
            copies[n]().wait_send()

    turned = acc[...].T.astype(stage.dtype)
    part = stage.shape[2]
    for side in range(2):
        for d in range(n_occ):
            at = (side * n_occ + d) * part
            stage[d, side] = turned[at : at + part]

    def occ_copy(to, source, d):
        return pltpu.make_async_remote_copy(
            src_ref=stage.at[to], dst_ref=out.at[pl.ds(2 * source, 2)],
            send_sem=occ_s.at[0, d], recv_sem=occ_s.at[1, d],
            device_id={"occ": to}, device_id_type=MESH,
        )

    for d in range(1, n_occ):
        occ_copy((o + d) % n_occ, o, d).start()
    mine = pltpu.make_async_copy(stage.at[o], out.at[pl.ds(2 * o, 2)], occ_s.at[0, 0])
    mine.start()
    for n in last:
        copies[n]().wait_send()
    mine.wait()
    for d in range(1, n_occ):
        occ_copy((o + d) % n_occ, o, d).wait_send()
        src = (o + n_occ - d) % n_occ
        occ_copy(src, src, d).wait_recv()


N_MESSAGES = 3 * NZ + (UP + DOWN) * (HALVES + NX) + 3


def on_device(integrals, occ_coeffs, virt_coeffs, block_ids, live_mask):
    blocks = integrals[0]
    n_i = occ_coeffs.shape[1]
    n_a = virt_coeffs.shape[1]
    n_occ = lax.axis_size("occ")
    bf16, f32 = jnp.bfloat16, jnp.float32
    wide = 2 * n_i
    ra, rb = CUT, ROWS - CUT
    any_space, smem = pl.BlockSpec(memory_space=pl.ANY), pl.BlockSpec(memory_space=pltpu.SMEM)
    got = pl.pallas_call(
        kernel,
        out_shape=jax.ShapeDtypeStruct((2 * n_occ, n_i // n_occ, n_a), bf16),
        in_specs=[smem, smem, any_space, any_space, any_space],
        out_specs=pl.BlockSpec(memory_space=pltpu.VMEM),
        scratch_shapes=[
            *(pltpu.VMEM(((hi - lo) * NX * GROUP, *blocks.shape[1:]), bf16) for lo, hi in FIRST),
            pltpu.VMEM((OWNERS * OWNED + 1, BS, n_i), bf16),
            pltpu.VMEM((n_a, OWNERS * ROWS), bf16),
            pltpu.VMEM((NZ, NX, ROWS, wide), bf16),
            pltpu.VMEM((NZ, NX, ROWS, wide), bf16),
            pltpu.VMEM((n_a, wide), f32),
            pltpu.VMEM((n_occ, 2, n_i // n_occ, n_a), bf16),
            pltpu.VMEM((NZ, ra, wide), bf16),
            pltpu.VMEM((NZ, ra, wide), bf16),
            pltpu.VMEM((NZ, ra, wide), bf16),
            pltpu.VMEM((UP, ra, wide), bf16),
            pltpu.VMEM((DOWN, ra, wide), bf16),
            pltpu.VMEM((UP, NX, rb, wide), bf16),
            pltpu.VMEM((DOWN, NX, rb, wide), bf16),
            pltpu.VMEM((3, rb, wide), bf16),
            pltpu.SemaphoreType.DMA((2, 2 * N_MESSAGES)),
            pltpu.SemaphoreType.DMA((2, n_occ)),
            pltpu.SemaphoreType.DMA((NZ + 2,)),
        ],
        compiler_params=pltpu.CompilerParams(
            collective_id=0, has_side_effects=True, vmem_limit_bytes=63_400_000
        ),
    )(
        block_ids,
        live_mask,
        blocks,
        occ_coeffs.reshape(OWNERS * OWNED, BS, n_i),
        virt_coeffs.T,
    )
    return jnp.transpose(got, (1, 0, 2))


def solution(mesh):
    return jax.shard_map(
        on_device,
        mesh=mesh,
        in_specs=(
            P("pair", None, None, "occ"),
            P(),
            P(None, "pair"),
            P(None, "pair", None),
            P("pair", None),
        ),
        out_specs=P("occ", None, "pair"),
        check_vma=False,
    )
```

time: 252 us -> 72 us (0.29)
  waiting for transfers between devices: 128 us -> 0 us
  Pallas kernels: 0 us -> 70.3 us
  local copies, waits for them, and re-layouts: 53.1 us -> 1.6 us
  starting transfers between devices: 20.4 us -> 0 us
  matrix products: 17.4 us -> 0 us
  between operations: 13.6 us -> 0.01 us
  blocking collectives: 12.4 us -> 0 us
  other arithmetic: 6.55 us -> 0 us
    all_gather x1 -> x0, waiting for transfers between devices: 84.2 us -> none  [on_device(): shard_piece = lax.all_gather(slab_sums, 'pair', axis=0, tiled=True)]
    pallas_call x0 -> x1, Pallas kernels: none -> 70.3 us  [on_device(): pl.pallas_call(kernel, out_shape=jax.ShapeDtypeStruct((2 * n_occ, n_i //...]
    all_to_all x2 -> x0, waiting for transfers between devices: 43.5 us -> none  [the longest x1 42.5 us: on_device(): lax.all_to_all(send_blocks, 'pair', split_axis=0, concat_axis=0, tiled=True)]
    all_to_all x2 -> x0, starting transfers between devices: 20.4 us -> none  [the longest x1 11.9 us: in_one_piece(): lax.all_to_all(both, axis, split_axis=split_dim, concat_axis=concat_dim,...]
    dot_general x3 -> x0, matrix products: 17.4 us -> none  [the longest x1 7.39 us: half_transform(): jnp.einsum('snqm,smi->snqi', shaped, coeff_rows, preferred_element_type=j...]
    all_to_all x1 -> x0, blocking collectives: 12.4 us -> none  [on_device(): lax.all_to_all(half_sums, 'occ', split_axis=3, concat_axis=2, tiled=True)]
    reshape x6 -> x0, local copies, waits for them, and re-layouts: 11 us -> none  [the longest x1 9.09 us: on_device(): shard_piece.reshape(piece_blocks * block_width, aux_count, slab_rows)]
    gather x9 -> x0, local copies, waits for them, and re-layouts: 10.7 us -> none  [the longest x1 4.35 us: on_device(): blocks[slot_index] * valid_flags[:, None, None].astype(jnp.bfloat16)]
  transfers between devices with their start and end apart: 3 -> 0, of which waited for: 3 -> 0; matrix products, arithmetic and copies ran while one was open for 5% -> 0% of each run, Pallas kernels for 0% -> 0%
where the time goes in v2:
time: 72 us; the launch traced here: 71.9 us
  Pallas kernels  70.3 us (98%)
  local copies, waits for them, and re-layouts  1.6 us (2%)
    pallas_call x1, Pallas kernels, on_device(): pl.pallas_call(kernel, out_shape=jax.ShapeDtypeStruct((2 * n_occ, n_i //...  70.3 us
    transpose x1, local copies, waits for them, and re-layouts, on_device(): return jnp.transpose(got, (1, 0, 2))  1.6 us

profile of v2, /device:TPU:1, one launch (start us, length us, event | category | flops | bytes accessed | tf_op | source)
XLA Modules:
  0.0 71.9 jit_solution(16763056790950306333)
XLA Ops:
  0.0 70.3 %shard_map.55 = bf16[16,16,160]{2,1,0:T(8,128)(2,1)} custom-call(s32[2,1,256]{2,1,0:T(1,128)} %ids.1, s32[1,256]{1,0:T(1,128)} %live.1, bf16[256,64,128]{2,1,0:T(8,128)(2,1)} %bitcast.4, bf16[96,64,128]{2,1,0:T(8,128)(2,1)} %bitcast.6, bf16[160,6144]{1,0:T(8,128)(2,1)} %bitcast.5), custom_call_target="tpu_custom_call" | custom-call | tf_op jit(solution)/shard_map/pallas_call | solution.py:410
  70.3 1.6 %copy.6 = bf16[16,16,160]{2,1,0:T(8,128)(2,1)} copy(bf16[16,16,160]{2,0,1:T(8,128)(2,1)} %bitcast.7) | data formatting | bytes 163840 | tf_op jit(solution)/shard_map/transpose | solution.py:445

commit v3 on v2

--- a/solution.py
+++ b/solution.py
@@ -17,8 +17,9 @@
 MESH = pl.DeviceIdType.MESH
 FIRST = ((0, 2), (2, 5), (5, 8))
 HALVES = 2
-
-RATE, LATENCY, HOP, WINDOW = 88e3, 1.25, 0.65, 1.5
+TOGETHER = 2
+
+RATE, LATENCY, HOP, WINDOW = 80e3, 1.25, 0.65, 1.0
 
 
 def far_first(k):
@@ -129,31 +130,30 @@
     load_c.wait()
 
     def transform(part, at, q):
-        on = [live[0, q * GROUP + j] for j in range(GROUP)]
-        seen, before = 0, []
-        for j in range(GROUP):
-            before.append(seen)
-            seen = seen + on[j]
+        slots = [0] * LIVE
+        on = [live[0, q * GROUP + j] != 0 for j in range(GROUP)]
+        for j in reversed(range(GROUP)):
+            slots = [jnp.where(on[j], new, old) for new, old in zip([j] + slots[:-1], slots)]
+        count = sum(jnp.where(t, 1, 0) for t in on)
         blocks, picks = [], [[] for _ in range(OWNED)]
-        for n in range(LIVE):
-            slot = 0
-            for j in range(1, GROUP):
-                slot = slot + jnp.where(jnp.logical_and(on[j] != 0, before[j] == n), j, 0)
+        for n, slot in enumerate(slots):
             mu, nu = ids[0, 0, q * GROUP + slot], ids[1, 0, q * GROUP + slot]
+            nu = jnp.where(count > n, nu, -1)
             blocks.append(part[at + slot])
             for b in range(OWNED):
-                hit = jnp.logical_and(seen > n, nu == q * OWNED + b)
-                picks[b].append(c[jnp.where(hit, mu, OWNERS * OWNED)])
+                picks[b].append(c[jnp.where(nu == q * OWNED + b, mu, OWNERS * OWNED)])
         left = [t[:, :BS] for t in blocks]
         right = [t[:, BS:] for t in blocks]
         lhs = jnp.concatenate(
             [jnp.concatenate(left, axis=1), jnp.concatenate(right, axis=1)], axis=0
         )
         rhs = jnp.concatenate([jnp.concatenate(p, axis=0) for p in picks], axis=1)
-        got = jnp.dot(lhs, rhs, preferred_element_type=jnp.float32).astype(s.dtype)
+        return jnp.dot(lhs, rhs, preferred_element_type=jnp.float32).astype(s.dtype)
+
+    def put(got, zz, xx):
         for b in range(OWNED):
             for side in range(2):
-                s[q // NX, q % NX, pl.ds(b * BS, BS), pl.ds(side * n_i, n_i)] = got[
+                s[zz, xx, pl.ds(b * BS, BS), pl.ds(side * n_i, n_i)] = got[
                     side * BS : (side + 1) * BS, b * n_i : (b + 1) * n_i
                 ]
 
@@ -203,10 +203,16 @@
             for k in range(lo, hi):
                 load_a(g, k).wait()
 
-            @pl.loop(0, (hi - lo) * NX)
-            def _(n):
-                q = zat(far_first(lo + n // NX)) * NX + n % NX
-                transform(parts[g], n * GROUP, q)
+            @pl.loop(lo, hi)
+            def _(k):
+                zz = zat(far_first(k))
+                for xx in range(0, NX, TOGETHER):
+                    got = [
+                        transform(parts[g], ((k - lo) * NX + xx + n) * GROUP, zz * NX + xx + n)
+                        for n in range(TOGETHER)
+                    ]
+                    for n in range(TOGETHER):
+                        put(got[n], zz, xx + n)
 
             if g == 0:
                 pl.semaphore_wait(barrier, 5 + n_occ - 1)

time: 72 us -> 66.7 us (0.926)
  Pallas kernels: 70.3 us -> 65 us
    pallas_call x1, Pallas kernels: 70.3 us -> 65 us  [on_device(): pl.pallas_call(kernel, out_shape=jax.ShapeDtypeStruct((2 * n_occ, n_i //...]
where the time goes in v3:
time: 66.7 us; the launch traced here: 66.6 us
  Pallas kernels  65 us (97%)
  local copies, waits for them, and re-layouts  1.6 us (2%)
    pallas_call x1, Pallas kernels, on_device(): pl.pallas_call(kernel, out_shape=jax.ShapeDtypeStruct((2 * n_occ, n_i //...  65 us
    transpose x1, local copies, waits for them, and re-layouts, on_device(): return jnp.transpose(got, (1, 0, 2))  1.6 us

profile of v3, /device:TPU:1, one launch (start us, length us, event | category | flops | bytes accessed | tf_op | source)
XLA Modules:
  0.0 66.6 jit_solution(7475766774911774970)
XLA Ops:
  0.0 65.0 %shard_map.55 = bf16[16,16,160]{2,1,0:T(8,128)(2,1)} custom-call(s32[2,1,256]{2,1,0:T(1,128)} %ids.1, s32[1,256]{1,0:T(1,128)} %live.1, bf16[256,64,128]{2,1,0:T(8,128)(2,1)} %bitcast.4, bf16[96,64,128]{2,1,0:T(8,128)(2,1)} %bitcast.6, bf16[160,6144]{1,0:T(8,128)(2,1)} %bitcast.5), custom_call_target="tpu_custom_call" | custom-call | tf_op jit(solution)/shard_map/pallas_call | solution.py:416
  65.0 1.6 %copy.6 = bf16[16,16,160]{2,1,0:T(8,128)(2,1)} copy(bf16[16,16,160]{2,0,1:T(8,128)(2,1)} %bitcast.7) | data formatting | bytes 163840 | tf_op jit(solution)/shard_map/transpose | solution.py:451

commit v4 on v3

--- a/solution.py
+++ b/solution.py
@@ -15,11 +15,12 @@
 CUT = 112
 UP, DOWN = NZ // 2, NZ // 2 - 1
 MESH = pl.DeviceIdType.MESH
-FIRST = ((0, 2), (2, 5), (5, 8))
+FIRST = ((0, 1), (1, 2), (2, 8))
 HALVES = 2
 TOGETHER = 2
 
-RATE, LATENCY, HOP, WINDOW = 80e3, 1.25, 0.65, 1.0
+RATE, LATENCY, HOP, WINDOW = 80000.0, 0.5, 0.65, 2.091
+LEAN = {'ax': -6.5, 'ax1': 31.9, 'ax2': -1.2, 'axm': -2.3, 'az': 30.0, 'azm': 10.6, 'b': -38.2, 'bz': 0.5, 'bzm': 6.9, 'clear': 0.7, 'gax0': 4.7, 'gax1': 32.0, 'gaxm': -14.0, 'gaz': 9.3, 'gazm': 20.1, 'gbz': 9.1, 'gbzm': -29.4, 'multiply': 13.1, 'own a': -24.3, 'own b': -19.8, 'transform': -55.9}
 
 
 def far_first(k):
@@ -48,6 +49,9 @@
             ranks[n] = by_name[n].cost + max([c + rank(f) for f, c in follow[n]], default=0.0)
         return ranks[n]
 
+    def lean(n):
+        return rank(n) + LEAN.get(n[0], 0.0)
+
     done, there, free, gone = {}, {}, {"x": 0.0, "z": 0.0}, {}
     now, left, out = 0.0, list(steps), []
     while left:
@@ -59,7 +63,7 @@
             at = max([at] + [free[link] - WINDOW for _, link, _, _ in s.sends])
             if at > now + 1e-9:
                 later.append(at)
-            elif best is None or rank(s.name) > rank(best.name):
+            elif best is None or lean(s.name) > lean(best.name):
                 best = s
         if best is None:
             now = min(later)
@@ -222,7 +226,7 @@
     for g, (lo, hi) in enumerate(FIRST):
         step(
             ready[lo], [("transform", g - 1)] if g else [], run=run_transform(g),
-            cost=0.55 * (hi - lo) + (2.0 if g == 0 else 0.0),
+            cost=0.35 * (hi - lo) + (1.8 if g == 0 else 0.0),
         )
 
     for k in range(NZ):
@@ -415,7 +419,7 @@
     any_space, smem = pl.BlockSpec(memory_space=pl.ANY), pl.BlockSpec(memory_space=pltpu.SMEM)
     got = pl.pallas_call(
         kernel,
-        out_shape=jax.ShapeDtypeStruct((2 * n_occ, n_i // n_occ, n_a), bf16),
+        out_shape=pltpu.VMEM((2 * n_occ, n_i // n_occ, n_a), bf16),
         in_specs=[smem, smem, any_space, any_space, any_space],
         out_specs=pl.BlockSpec(memory_space=pltpu.VMEM),
         scratch_shapes=[
@@ -439,7 +443,7 @@
             pltpu.SemaphoreType.DMA((NZ + 2,)),
         ],
         compiler_params=pltpu.CompilerParams(
-            collective_id=0, has_side_effects=True, vmem_limit_bytes=63_400_000
+            collective_id=0, has_side_effects=True, vmem_limit_bytes=63_200_000
         ),
     )(
         block_ids,

time: 66.7 us -> 63.8 us (0.957)
  Pallas kernels: 65 us -> 63 us
  local copies, waits for them, and re-layouts: 1.6 us -> 0.7 us
    pallas_call x1, Pallas kernels: 65 us -> 63 us  [on_device(): pl.pallas_call(kernel, out_shape=pltpu.VMEM((2 * n_occ, n_i // n_occ, n_a...]
    transpose x1, local copies, waits for them, and re-layouts: 1.6 us -> 0.7 us  [on_device(): return jnp.transpose(got, (1, 0, 2))]
where the time goes in v4:
time: 63.8 us; the launch traced here: 63.7 us
  Pallas kernels  63 us (99%)
  local copies, waits for them, and re-layouts  0.7 us (1%)
    pallas_call x1, Pallas kernels, on_device(): pl.pallas_call(kernel, out_shape=pltpu.VMEM((2 * n_occ, n_i // n_occ, n_a...  63 us

profile of v4, /device:TPU:1, one launch (start us, length us, event | category | flops | bytes accessed | tf_op | source)
XLA Modules:
  0.0 63.7 jit_solution(11394837680618953438)
XLA Ops:
  0.0 63.0 %shard_map.55 = bf16[16,16,160]{2,1,0:T(8,128)(2,1)S(1)} custom-call(s32[2,1,256]{2,1,0:T(1,128)} %ids.1, s32[1,256]{1,0:T(1,128)} %live.1, bf16[256,64,128]{2,1,0:T(8,128)(2,1)} %bitcast.5, bf16[96,64,128]{2,1,0:T(8,128)(2,1)} %bitcast.7, bf16[160,6144]{1,0:T(8,128)(2,1)} %bitcast.6), custom_call_target="tpu_custom_call" | custom-call | tf_op jit(solution)/shard_map/pallas_call | solution.py:420
  63.0 0.7 %copy.6 = bf16[16,16,160]{2,1,0:T(8,128)(2,1)} copy(bf16[16,16,160]{2,0,1:T(8,128)(2,1)S(1)} %bitcast.4) | data formatting | bytes 163840 | tf_op jit(solution)/shard_map/transpose | solution.py:455

commit v5 on v4

--- a/solution.py
+++ b/solution.py
@@ -15,12 +15,12 @@
 CUT = 112
 UP, DOWN = NZ // 2, NZ // 2 - 1
 MESH = pl.DeviceIdType.MESH
-FIRST = ((0, 1), (1, 2), (2, 8))
+FIRST = ((0, 2), (2, 5), (5, 8))
 HALVES = 2
 TOGETHER = 2
 
-RATE, LATENCY, HOP, WINDOW = 80000.0, 0.5, 0.65, 2.091
-LEAN = {'ax': -6.5, 'ax1': 31.9, 'ax2': -1.2, 'axm': -2.3, 'az': 30.0, 'azm': 10.6, 'b': -38.2, 'bz': 0.5, 'bzm': 6.9, 'clear': 0.7, 'gax0': 4.7, 'gax1': 32.0, 'gaxm': -14.0, 'gaz': 9.3, 'gazm': 20.1, 'gbz': 9.1, 'gbzm': -29.4, 'multiply': 13.1, 'own a': -24.3, 'own b': -19.8, 'transform': -55.9}
+RATE, LATENCY, HOP, WINDOW = 80000.0, 1.416, 0.65, 1.455
+LEAN = {'ax': 15.1, 'ax1': 14.0, 'ax2': 3.5, 'axm': 5.6, 'az': -13.3, 'azm': -0.4, 'b': 40.3, 'bz': -14.2, 'bzm': -14.3, 'clear': -4.3, 'gax0': -11.3, 'gax1': 57.5, 'gaxm': -23.6, 'gaz': 118.3, 'gazm': -12.0, 'gbz': 27.5, 'gbzm': -25.4, 'multiply': -23.5, 'own a': -38.5, 'own b': 27.6, 'transform': -45.5}
 
 
 def far_first(k):
@@ -186,6 +186,7 @@
         return 0.05 + size / 4e5
 
     def step(name, after=(), needs=(), sends=(), run=lambda: None, cost=start_cost):
+        cost += 0.02 * (1 + len(needs) + len(sends))
         steps.append(Step(name, cost, list(after), list(needs), list(sends), run))
 
     def add(at, *terms, into=s):

time: 63.8 us -> 63 us (0.987)
  Pallas kernels: 63 us -> 62.2 us
    pallas_call x1, Pallas kernels: 63 us -> 62.2 us  [on_device(): pl.pallas_call(kernel, out_shape=pltpu.VMEM((2 * n_occ, n_i // n_occ, n_a...]
where the time goes in v5:
time: 63 us; the launch traced here: 62.9 us
  Pallas kernels  62.2 us (99%)
  local copies, waits for them, and re-layouts  0.7 us (1%)
    pallas_call x1, Pallas kernels, on_device(): pl.pallas_call(kernel, out_shape=pltpu.VMEM((2 * n_occ, n_i // n_occ, n_a...  62.2 us

profile of v5, /device:TPU:1, one launch (start us, length us, event | category | flops | bytes accessed | tf_op | source)
XLA Modules:
  0.0 62.9 jit_solution(17858940987468898146)
XLA Ops:
  0.0 62.2 %shard_map.55 = bf16[16,16,160]{2,1,0:T(8,128)(2,1)S(1)} custom-call(s32[2,1,256]{2,1,0:T(1,128)} %ids.1, s32[1,256]{1,0:T(1,128)} %live.1, bf16[256,64,128]{2,1,0:T(8,128)(2,1)} %bitcast.5, bf16[96,64,128]{2,1,0:T(8,128)(2,1)} %bitcast.7, bf16[160,6144]{1,0:T(8,128)(2,1)} %bitcast.6), custom_call_target="tpu_custom_call" | custom-call | tf_op jit(solution)/shard_map/pallas_call | solution.py:421
  62.2 0.7 %copy.6 = bf16[16,16,160]{2,1,0:T(8,128)(2,1)} copy(bf16[16,16,160]{2,0,1:T(8,128)(2,1)S(1)} %bitcast.4) | data formatting | bytes 163840 | tf_op jit(solution)/shard_map/transpose | solution.py:456
